TPU v7x, 32 devices: a whole 2x2x4 slice. The times are simulated.
32 devices in a mesh: dp: 8 (over z, x), mp: 4 (over y, core).
Axes of the slice: x: 2, y: 2, z: 4, core: 2. Of those that a mesh axis runs over, the one named last changes fastest.
Arguments:
- tokens: bfloat16 [16384, 768], P('dp'), may hold values from -6 to 6
- cotangent: bfloat16 [16384, 768], P('dp'), may hold values from -6 to 6
- qkv_weight: bfloat16 [3, 768, 768], P(None, None, 'mp'), may hold values from -0.21875 to 0.21875
- col_bias: bfloat16 [2, 768], P(None, 'mp'), may hold values from -3 to 3
- out_weight: bfloat16 [768, 768], P('mp'), may hold values from -1.75 to 1.75
- in_weight: bfloat16 [768, 3072], P(None, 'mp'), may hold values from -0.21875 to 0.21875
- in_bias: bfloat16 [3072], P('mp'), may hold values from -3 to 3
- down_weight: bfloat16 [3072, 768], P('mp'), may hold values from -0.109375 to 0.109375
- vectors: bfloat16 [6, 768], replicated, may hold values from 0.5 to 1.5
- slot_is_long: int32 [32], P('dp'), may hold values from 0 to 1
- seq_len: int32 [32, 4], P('dp'), may hold values from 1 to 128, as said below
- master: float32 [4, 8, 221472], P('mp', 'dp'), may hold values from -0.18 to 0.18
- first_moment: float32 [4, 8, 221472], P('mp', 'dp'), as said below
- second_moment: float32 [4, 8, 221472], P('mp', 'dp'), as said below
- average: float32 [4, 8, 221472], P('mp', 'dp'), may hold values from -0.18 to 0.18
Outputs:
- output: bfloat16 [16384, 768], P('dp')
- grad_input: float32 [16384, 768], P('dp')
- vector_grad: float32 [4, 8, 144], P('mp', 'dp')
- new_master: float32 [4, 8, 221472], P('mp', 'dp')
- new_first: float32 [4, 8, 221472], P('mp', 'dp')
- new_second: float32 [4, 8, 221472], P('mp', 'dp')
- new_average: float32 [4, 8, 221472], P('mp', 'dp')
Inputs may be any that keep to these rules, and one draw needn't show every extreme that they name: `seq_len`: in every slot one of the four entries equals 128. `first_moment`: entries of both signs, none near zero. `second_moment`: every entry positive.
All inputs are finite; a program needn't handle non-finite values.
Results may differ from a plain program's by a relative error of at most 0.02.
Values may be sent and summed in bfloat16 or wider, within the bound.
No kernel may reach another device: no remote copies, remote signals or barrier semaphores. Data moves between devices by JAX's collectives and lax.ppermute only.
A program may use at most 128 MiB of HBM per device.

v0:
```python
import jax
import jax.numpy as jnp
from jax import lax
from jax.sharding import PartitionSpec as P

HDIM = 64
SLOT_TOKENS = 512
SHORT_TOKENS = 128
STEP = 3
NORM_EPS = 1e-12


def slot_masks(kind, sequence_lengths):
    pos = jnp.arange(SLOT_TOKENS, dtype=jnp.int32)
    block = pos // SHORT_TOKENS
    is_long = kind == 1
    segment = jnp.where(is_long, 0, block)
    inner = jnp.where(is_long, pos, pos % SHORT_TOKENS)
    picks = block[:, None] == jnp.arange(sequence_lengths.shape[0], dtype=jnp.int32)[None, :]
    short_len = jnp.sum(jnp.where(picks, sequence_lengths[None, :], 0), axis=1)
    seg_len = jnp.where(is_long, jnp.sum(sequence_lengths), short_len)
    valid = inner < seg_len
    allowed = (segment[:, None] == segment[None, :]) & valid[None, :]
    key_ok = jnp.arange(SHORT_TOKENS, dtype=jnp.int32)[None, :] < sequence_lengths[:, None]
    return (allowed, valid, key_ok)


def layer_norm(z, gain, shift):
    centered = z - jnp.mean(z, axis=-1, keepdims=True)
    var = jnp.mean(centered * centered, axis=-1, keepdims=True)
    return centered * lax.rsqrt(var + NORM_EPS) * gain + shift


def gelu_exact(u):
    return 0.5 * u * (1.0 + jax.scipy.special.erf(u * 2.0 ** (-0.5)))


def block_scores(query, keys, mask):
    scores = jnp.einsum("bqhe,bkhe->bhqk", query, keys, preferred_element_type=jnp.float32)
    return jnp.where(mask[:, None], scores, -1000000000.0)


def attend_blocks(query, keys, values, mask):
    scores = block_scores(query, keys, mask)
    top = jnp.max(scores, axis=-1, keepdims=True)
    expd = jnp.exp(scores - top)
    total = jnp.sum(expd, axis=-1, keepdims=True)
    probs = expd / total
    lse = top[..., 0] + jnp.log(total[..., 0])
    context = jnp.einsum(
        "bhqk,bkhe->bqhe", probs.astype(jnp.bfloat16), values, preferred_element_type=jnp.float32
    )
    return (context, lse)


def attend_back(query, keys, values, dctx, lse, mask):
    scores = block_scores(query, keys, mask)
    probs = jnp.where(mask[:, None], jnp.exp(scores - lse[..., None]), 0.0)
    dprob = jnp.einsum("bqhe,bkhe->bhqk", dctx, values, preferred_element_type=jnp.float32)
    dscore = probs * (dprob - jnp.sum(probs * dprob, axis=-1, keepdims=True))
    dscore_b = dscore.astype(jnp.bfloat16)
    d_query = jnp.einsum("bhqk,bkhe->bqhe", dscore_b, keys, preferred_element_type=jnp.float32)
    d_keys = jnp.einsum("bhqk,bqhe->bkhe", dscore_b, query, preferred_element_type=jnp.float32)
    d_values = jnp.einsum(
        "bhqk,bqhe->bkhe", probs.astype(jnp.bfloat16), dctx, preferred_element_type=jnp.float32
    )
    return (
        d_query.astype(jnp.bfloat16),
        d_keys.astype(jnp.bfloat16),
        d_values.astype(jnp.bfloat16),
    )


def slot_forward(item):
    query, keys, values, kind, sequence_lengths = item
    allowed, valid, key_ok = slot_masks(kind, sequence_lengths)

    def whole():
        context, lse = attend_blocks(query[None], keys[None], values[None], allowed[None])
        return (context[0], lse[0])

    return whole()


def slot_backward(item):
    query, keys, values, dctx, lse, kind, sequence_lengths = item
    allowed, valid, key_ok = slot_masks(kind, sequence_lengths)

    def whole():
        grads = attend_back(
            query[None], keys[None], values[None], dctx[None], lse[None], allowed[None]
        )
        return tuple((g[0] for g in grads))

    return whole()


def body(
    tokens,
    cotangent,
    qkv_weight,
    col_bias,
    out_weight,
    in_weight,
    in_bias,
    down_weight,
    vectors,
    slot_is_long,
    seq_len,
    master,
    first_moment,
    second_moment,
    average,
):
    rows = tokens.shape[0]
    slots = slot_is_long.shape[0]
    heads_here = qkv_weight.shape[2] // HDIM
    scale = HDIM ** (-0.5)
    ndata = lax.axis_size("dp")
    nmodel = lax.axis_size("mp")
    vec = vectors.astype(jnp.float32)
    bias = col_bias.astype(jnp.float32)
    proj = jnp.einsum("td,cde->cte", tokens, qkv_weight, preferred_element_type=jnp.float32)
    query = ((proj[0] + bias[0]) * scale).astype(jnp.bfloat16)
    keys = proj[1].astype(jnp.bfloat16)
    values = (proj[2] + bias[1]).astype(jnp.bfloat16)
    shape4 = (slots, SLOT_TOKENS, heads_here, HDIM)
    query4 = query.reshape(shape4)
    keys4 = keys.reshape(shape4)
    values4 = values.reshape(shape4)
    context, lse = lax.map(slot_forward, (query4, keys4, values4, slot_is_long, seq_len))
    context_b = context.reshape(rows, -1).astype(jnp.bfloat16)
    attn_part = jnp.dot(context_b, out_weight, preferred_element_type=jnp.float32).astype(
        jnp.bfloat16
    )
    attn = lax.psum(attn_part, "mp").astype(jnp.float32)
    z_one = tokens.astype(jnp.float32) + attn + vec[4]
    x_one, norm_one_pull = jax.vjp(layer_norm, z_one, vec[0], vec[1])
    x_one_b = x_one.astype(jnp.bfloat16)
    pre = jnp.dot(x_one_b, in_weight, preferred_element_type=jnp.float32) + in_bias.astype(
        jnp.float32
    )
    hidden, gelu_pull = jax.vjp(gelu_exact, pre)
    hidden_b = hidden.astype(jnp.bfloat16)
    down_part = jnp.dot(hidden_b, down_weight, preferred_element_type=jnp.float32).astype(
        jnp.bfloat16
    )
    ffn = lax.psum(down_part, "mp").astype(jnp.float32)
    z_two = x_one + ffn + vec[5]
    output, norm_two_pull = jax.vjp(layer_norm, z_two, vec[2], vec[3])
    valid = jax.vmap(lambda kk, ll: slot_masks(kk, ll)[1])(slot_is_long, seq_len).reshape(rows)
    grad_out = cotangent.astype(jnp.float32) * valid[:, None].astype(jnp.float32)
    dz_two, d_gain_two, d_shift_two = norm_two_pull(grad_out)
    d_bias_two = jnp.sum(dz_two, axis=0)
    dz_two_b = dz_two.astype(jnp.bfloat16)
    g_down = jnp.dot(hidden_b.T, dz_two_b, preferred_element_type=jnp.float32)
    d_hidden = jnp.dot(dz_two_b, down_weight.T, preferred_element_type=jnp.float32)
    d_pre = gelu_pull(d_hidden)[0]
    d_pre_b = d_pre.astype(jnp.bfloat16)
    g_in = jnp.dot(x_one_b.T, d_pre_b, preferred_element_type=jnp.float32)
    g_inb = jnp.sum(d_pre_b.astype(jnp.float32), axis=0)
    ffn_pieces = (g_in.reshape(ndata, -1), g_down.reshape(ndata, -1), g_inb.reshape(ndata, -1))
    back_one = jnp.dot(d_pre_b, in_weight.T, preferred_element_type=jnp.float32).astype(
        jnp.bfloat16
    )
    dx_one = dz_two + lax.psum(back_one, "mp").astype(jnp.float32)
    dz_one, d_gain_one, d_shift_one = norm_one_pull(dx_one)
    d_bias_out = jnp.sum(dz_one, axis=0)
    dz_one_b = dz_one.astype(jnp.bfloat16)
    g_out = jnp.dot(context_b.T, dz_one_b, preferred_element_type=jnp.float32)
    d_context = jnp.dot(dz_one_b, out_weight.T, preferred_element_type=jnp.float32).astype(
        jnp.bfloat16
    )
    d_query, d_keys, d_values = lax.map(
        slot_backward,
        (query4, keys4, values4, d_context.reshape(shape4), lse, slot_is_long, seq_len),
    )
    d_query = d_query.reshape(rows, -1)
    d_keys = d_keys.reshape(rows, -1)
    d_values = d_values.reshape(rows, -1)
    d_proj = jnp.stack([d_query, d_keys, d_values])
    factors = jnp.array([scale, 1.0, 1.0], jnp.float32)[:, None, None]
    g_qkv = jnp.einsum("td,cte->cde", tokens, d_proj, preferred_element_type=jnp.float32) * factors
    g_col = jnp.stack(
        [
            jnp.sum(d_query.astype(jnp.float32), axis=0) * scale,
            jnp.sum(d_values.astype(jnp.float32), axis=0),
        ]
    )
    back_zero = (
        jnp.dot(d_query, qkv_weight[0].T, preferred_element_type=jnp.float32) * scale
        + jnp.dot(d_keys, qkv_weight[1].T, preferred_element_type=jnp.float32)
        + jnp.dot(d_values, qkv_weight[2].T, preferred_element_type=jnp.float32)
    ).astype(jnp.bfloat16)
    grad_input = dz_one + lax.psum(back_zero, "mp").astype(jnp.float32)
    g_vec = jnp.stack(
        [d_gain_one, d_shift_one, d_gain_two, d_shift_two, d_bias_out, d_bias_two]
    ).reshape(-1)
    share = g_vec.shape[0] // nmodel
    g_vec_mine = lax.dynamic_slice_in_dim(g_vec, lax.axis_index("mp") * share, share)
    attn_pieces = (
        g_qkv.reshape(ndata, -1),
        g_out.reshape(ndata, -1),
        g_col.reshape(ndata, -1),
        g_vec_mine.reshape(ndata, -1),
    )
    summed = (
        lax.psum_scatter(attn_pieces[0], "dp", scatter_dimension=0, tiled=True),
        lax.psum_scatter(attn_pieces[1], "dp", scatter_dimension=0, tiled=True),
        lax.psum_scatter(ffn_pieces[0], "dp", scatter_dimension=0, tiled=True),
        lax.psum_scatter(ffn_pieces[1], "dp", scatter_dimension=0, tiled=True),
        lax.psum_scatter(attn_pieces[2], "dp", scatter_dimension=0, tiled=True),
        lax.psum_scatter(ffn_pieces[2], "dp", scatter_dimension=0, tiled=True),
        lax.psum_scatter(attn_pieces[3], "dp", scatter_dimension=0, tiled=True),
    )
    grad = (jnp.concatenate(summed, axis=1) / ndata).reshape(master.shape)
    vector_grad = (summed[6] / ndata).reshape(1, 1, -1)
    new_first = 0.5 * first_moment + 0.5 * grad
    new_second = 0.5 * second_moment + 0.5 * grad * grad
    corr = 1.0 - 0.5**STEP
    new_master = master - 0.02 * (
        new_first / corr / (jnp.sqrt(new_second / corr) + 1e-08) + 0.01 * master
    )
    new_average = 0.75 * average + 0.25 * new_master
    return (
        output.astype(jnp.bfloat16),
        grad_input,
        vector_grad,
        new_master,
        new_first,
        new_second,
        new_average,
    )


def solution(mesh):
    placed = (
        P("dp", None),
        P("dp", None),
        P(None, None, "mp"),
        P(None, "mp"),
        P("mp", None),
        P(None, "mp"),
        P("mp"),
        P("mp", None),
        P(),
        P("dp"),
        P("dp", None),
        P("mp", "dp", None),
        P("mp", "dp", None),
        P("mp", "dp", None),
        P("mp", "dp", None),
    )
    return jax.shard_map(
        body,
        mesh=mesh,
        in_specs=placed,
        out_specs=(
            P("dp", None),
            P("dp", None),
            P("mp", "dp", None),
            P("mp", "dp", None),
            P("mp", "dp", None),
            P("mp", "dp", None),
            P("mp", "dp", None),
        ),
        check_vma=False,
    )
```

profile of v0, /device:TPU:0, one launch (start us, length us, event | category | flops | bytes accessed | tf_op | source)
XLA Modules:
  0.0 723.3 jit_solution(13496758862264162872)
XLA Ops:
  7.2 4.3 convolution_bitcast_fusion
  13.1 3.1 squeeze.43
  16.2 2.2 squeeze.44
  19.4 2.9 fusion.85
  22.3 28.6 %while.30 = (s32[]{:T(128)}, bf16[4,512,3,64]{1,3,2,0:T(8,128)(2,1)}, f32[4,3,512]{2,1,0:T(4,128)}, bf16[4,512,3,64]{1,3,2,0:T(8,128)(2,1)S(1)}, s32[4]{0:T(128)...) while((s32[]{:T(128)}, ...), condition=%wide.region_5.6_spmd, body=%wide.region_0.5_spmd.sunk | while | flops 208942080 | bytes 11540152 | solution.py:131
  27.8 1.7 fusion.169
  35.0 1.6 fusion.169
  42.1 1.7 fusion.169
  50.9 2.0 copy.76
  53.2 3.7 convolution_convert_fusion.4
  58.3 69.8 %all-reduce.15.cloned.1.call-done = bf16[2048,768]{1,0:T(8,128)(2,1)} async-done(((bf16[2048,768]{1,0:T(8,128)(2,1)}), bf16[2048,768]{1,0:T(8,128)(2,1)}) %all-reduce.15.cloned.1.call-update) | async-done | bytes 3145744 | tf_op jit(solution)/shard_map/psum | solution.py:136
  128.2 4.1 fusion.74
  132.9 1.8 multiply_reduce_fusion.6
  135.3 6.7 multiply_convert_fusion.1
  142.0 1.7 copy-done.45
  143.6 3.9 convolution_convert_fusion.3
  151.7 64.5 %all-reduce.17.cloned.1.call-done = bf16[2048,768]{1,0:T(8,128)(2,1)} async-done(((bf16[2048,768]{1,0:T(8,128)(2,1)}), bf16[2048,768]{1,0:T(8,128)(2,1)}) %all-reduce.17.cloned.1.call-update) | async-done | bytes 3145744 | tf_op jit(solution)/shard_map/psum | solution.py:148
  216.3 5.4 fusion.126
  223.6 3.6 multiply_reduce_fusion.1
  227.3 4.7 fusion.125
  232.1 6.4 convert_reduce_fusion
  240.1 4.0 convolution_convert_fusion.2
  244.6 7.9 %fusion.114 = f32[768,768]{1,0:T(8,128)} fusion(bf16[2048,768]{1,0:T(8,128)(2,1)} %copy-done.45, f32[2048,768]{1,0:T(8,128)} %copy-done.7, f32[2048]{0:T(1024)} %copy-done.21), kind=kOutput, calls=%fused_computation.207 | convolution fusion | flops 2419064832 | bytes 11804672 | tf_op jit(solution)/shard_map/dot_general | solution.py:156
  252.5 3.5 reshape.870
  256.0 56.8 %all-reduce.19.cloned.1.call-done = bf16[2048,768]{1,0:T(8,128)(2,1)} async-done(((bf16[2048,768]{1,0:T(8,128)(2,1)}), bf16[2048,768]{1,0:T(8,128)(2,1)}) %all-reduce.19.cloned.1.call-update) | async-done | bytes 3145744 | tf_op jit(solution)/shard_map/psum | solution.py:166
  312.8 9.4 %multiply_reduce_fusion.2 = (f32[768]{0:T(1024)S(1)}, f32[2048]{0:T(1024)S(1)}, f32[768]{0:T(1024)S(1)}, f32[768]{0:T(1024)S(1)}) fusion(f32[2048]{0:T(1024)S(1)} %copy-done.18, bf16[2048,768]{1,0:T(8,128)(2,1)} %all-reduce.19.cloned.1.call-done, f32[2048,768]{1,0:T(8,128)} %copy-done.7, f32[2048]{0:T(1024)S(1)} %copy-done.22, ...), kind=kLoop, calls=%fused_computation.97 | loop fusion | flops 25161472 | bytes 15776768 | tf_op jit(solution)/shard_map/transpose(jvp())/reduce_sum | solution.py:31
  322.3 6.0 fusion.124
  328.4 2.7 copy-done.2
  335.1 46.2 %while.31 = (s32[]{:T(128)}, bf16[4,512,3,64]{1,3,2,0:T(8,128)(2,1)}, bf16[4,512,3,64]{1,3,2,0:T(8,128)(2,1)}, bf16[4,512,3,64]{1,3,2,0:T(8,128)(2,1)}, bf16[4,5...) while((s32[]{:T(128)}, ...), condition=%wide.region_23.24_spmd, body=%wide.region_19.23_spmd.sunk | while | flops 511226880 | bytes 26134740 | solution.py:174
  381.4 1.8 copy.80
  383.2 1.7 copy.81
  385.0 1.7 copy.79
  389.4 2.8 add_convert_fusion
  392.3 8.5 %fusion.117 = f32[768,768]{1,0:T(8,128)} fusion(bf16[2048,768]{1,0:T(8,128)(2,1)} %copy-done.44, f32[768]{0:T(1024)S(1)} %copy-done.30, f32[768]{0:T(1024)S(1)} %get-tuple-element.346, f32[2048]{0:T(1024)S(1)} %copy-done.18, bf16[2048,768]{1,0:T(8,128)(2,1)} %all-reduce.15.cloned.1.call-done, bf16[2048,768]{1,0:T(8,128)(2,1)} %param.20, ...), kind=kOutput, calls=%fused_computation.210 | convolution fusion | flops 2430074880 | bytes 11822080 | tf_op jit(solution)/shard_map/dot_general | solution.py:160
  400.8 3.5 reshape.869
  408.7 3.9 fusion.116
  413.6 5.4 multiply_bitcast_fusion
  419.0 1.9 copy.85
  421.0 2.2 reshape.867
  425.7 35.2 %all-reduce.21.cloned.1.call-done = bf16[2048,768]{1,0:T(8,128)(2,1)} async-done(((bf16[2048,768]{1,0:T(8,128)(2,1)}), bf16[2048,768]{1,0:T(8,128)(2,1)}) %all-reduce.21.cloned.1.call-update) | async-done | bytes 3145744 | tf_op jit(solution)/shard_map/psum | solution.py:195
  460.9 6.0 add_reduce_fusion
  467.1 39.8 %all-reduce.7 = (f32[8,144]{1,0:T(8,128)S(1)}, f32[8,48]{1,0:T(8,128)S(1)}, f32[8,96]{1,0:T(8,128)S(1)}) all-reduce(f32[8,144]{1,0:T(8,128)S(1)} %reshape.865, f32[8,48]{1,0:T(8,128)S(1)} %reshape.871, f32[8,96]{1,0:T(8,128)S(1)} %reshape.872), channel_id=2, replica_groups=mesh['dp'=8,'mp'=4] {'dp'}, use_global_device_ids=true, to_apply=%region_31.32.clone | all-reduce | flops 2304 | bytes 18432
  509.4 188.2 %all-reduce.23.cloned.1.call-done = (f32[8,55296]{1,0:T(8,128)}, f32[8,18432]{1,0:T(8,128)}, f32[8,73728]{1,0:T(8,128)}, f32[8,73728]{1,0:T(8,128)}) async-done(((f32[8,55296]{1,0:T(8,128)}, f32[8,18432]{1,0:T(8,128)}, f32[8,73728]{1,0:T(8,128)}, f32[8,73728]{1,0:T(8,128)}), (f32[8,55296]{1,0:T(8,128)}, f32[8,18432]{1,0:T(8,128)}, f32[8,73728]{1,0:T(8,128)}, ...) | async-done | bytes 7077904
  697.6 2.3 fusion.101
  699.9 1.8 fusion.102
  701.6 2.5 fusion.92
  704.2 2.5 fusion.91
  707.4 9.2 %multiply_add_fusion.1 = (f32[1,1,221472]{2,1,0:T(1,128)}, f32[1,1,221472]{2,1,0:T(1,128)}, f32[1,1,221472]{2,1,0:T(1,128)}, f32[1,1,221472]{2,1,0:T(1,128)}) fusion(f32[1,1,221472]{2,1,0:T(1,128)S(1)} %copy-done.13, f32[1,1,221472]{2,1,0:T(1,128)} %param.31, f32[1,1,221472]{2,1,0:T(1,128)S(1)} %dynamic-update-slice.6, f32[1,1,221472]{2,1,0:T(1,128)} %param.32, ...), kind=kLoop, calls=%fused_computation.144 | loop fusion | flops 3986496 | bytes 7972992 | tf_op jit(solution)/shard_map/add | solution.py:224
  (265 shorter events, 95.8 us)
Async XLA Ops:
  7.2 128.1 %copy-start = (bf16[768,768]{1,0:T(8,128)(2,1)S(1)}, bf16[768,768]{1,0:T(8,128)(2,1)}, u32[]{:S(2)}) copy-start(bf16[768,768]{1,0:T(8,128)(2,1)} %param.25) | copy-start | bytes 3538948
  7.2 121.0 %all-reduce.15.cloned.1.call-start = ((), (), s32[]{:S(2)}) async-start(), calls=%async_computation | async-start | bytes 6291456 | tf_op jit(solution)/shard_map/psum | solution.py:136
  11.5 6.9 copy-start.37
  16.2 6.1 copy-start.40
  50.9 2.0 copy-start.10
  53.0 4.1 copy-start.32
  53.0 4.1 copy-start.36
  56.9 159.4 %all-reduce.17.cloned.1.call-start = ((), (), s32[]{:S(2)}) async-start(), calls=%async_computation.1 | async-start | bytes 6291456 | tf_op jit(solution)/shard_map/psum | solution.py:148
  128.2 4.1 copy-start.3
  128.2 4.7 copy-start.5
  128.2 7.1 copy-start.29
  128.2 7.1 copy-start.33
  135.3 6.7 copy-start.17
  135.3 8.4 %copy-start.38 = (bf16[768,768]{1,0:T(8,128)(2,1)S(1)}, bf16[768,768]{1,0:T(8,128)(2,1)}, u32[]{:S(2)}) copy-start(bf16[768,768]{1,0:T(8,128)(2,1)} %param.27) | copy-start | bytes 3538948
  147.6 165.2 %all-reduce.19.cloned.1.call-start = ((), (), s32[]{:S(2)}) async-start(), calls=%async_computation.2 | async-start | bytes 6291456 | tf_op jit(solution)/shard_map/psum | solution.py:166
  221.7 1.9 copy-start.9
  222.6 4.6 copy-start.31
  223.6 8.4 %slice-start = ((s8[6291456]{0:T(1024)(128)(4,1)}), s8[4194304]{0:T(1024)(128)(4,1)S(1)}, s32[]{:S(2)}) async-start(s8[6291456]{0:T(1024)(128)(4,1)} %bitcast.220), calls=%async_computation.5 | async-start | bytes 8388608
  227.3 4.8 copy-start.34
  227.3 4.8 copy-start.39
  227.3 4.8 slice-start.1
  232.0 6.4 copy-start.7
  232.0 6.4 copy-start.21
  244.1 216.8 %all-reduce.21.cloned.1.call-start = ((), (), s32[]{:S(2)}) async-start(), calls=%async_computation.3 | async-start | bytes 6291456 | tf_op jit(solution)/shard_map/psum | solution.py:195
  244.6 68.2 %copy-start.18 = (f32[2048]{0:T(1024)S(1)}, f32[2048]{0:T(1024)}, u32[]{:S(2)}) copy-start(f32[2048]{0:T(1024)} %copy-done.17) | copy-start | bytes 24580
  244.6 68.2 %copy-start.22 = (f32[2048]{0:T(1024)S(1)}, f32[2048]{0:T(1024)}, u32[]{:S(2)}) copy-start(f32[2048]{0:T(1024)} %copy-done.21) | copy-start | bytes 24580
  256.0 66.2 %copy-start.25 = (f32[2048]{0:T(1024)S(1)}, f32[2048]{0:T(1024)}, u32[]{:S(2)}) copy-start(f32[2048]{0:T(1024)} %copy-done.24) | copy-start | bytes 24580
  312.8 9.4 %copy-start.4 = (bf16[2048,768]{1,0:T(8,128)(2,1)S(1)}, bf16[2048,768]{1,0:T(8,128)(2,1)}, u32[]{:S(2)}) copy-start(bf16[2048,768]{1,0:T(8,128)(2,1)} %param.20) | copy-start | bytes 9437188
  312.8 9.4 %copy-start.6 = (bf16[2048,768]{1,0:T(8,128)(2,1)S(1)}, bf16[2048,768]{1,0:T(8,128)(2,1)}, u32[]{:S(2)}) copy-start(bf16[2048,768]{1,0:T(8,128)(2,1)} %all-reduce.15.cloned.1.call-done) | copy-start | bytes 9437188
  312.8 9.4 %copy-start.8 = (bf16[2048,768]{1,0:T(8,128)(2,1)S(1)}, bf16[2048,768]{1,0:T(8,128)(2,1)}, u32[]{:S(2)}) copy-start(bf16[2048,768]{1,0:T(8,128)(2,1)} %all-reduce.19.cloned.1.call-done) | copy-start | bytes 9437188
  322.3 8.8 %copy-start.12 = (bf16[192,768]{1,0:T(8,128)(2,1)S(1)}, bf16[192,768]{1,0:T(8,128)(2,1)}, u32[]{:S(2)}) copy-start(bf16[192,768]{1,0:T(8,128)(2,1)} %param.24) | copy-start | bytes 884740
  328.3 2.7 copy-start.2
  328.3 6.8 copy-start.41
  328.4 80.3 %copy-start.19 = (f32[2048]{0:T(1024)}, f32[2048]{0:T(1024)S(1)}, u32[]{:S(2)}) copy-start(f32[2048]{0:T(1024)S(1)} %negate_multiply_fusion) | copy-start | bytes 24580
  381.4 5.5 copy-start.14
  389.4 2.9 copy-start.30
  392.2 305.4 %all-reduce.23.cloned.1.call-start = ((), (), s32[]{:S(2)}) async-start(), calls=%async_computation.4 | async-start | bytes 14155776
  405.8 7.8 %copy-start.43 = (f32[3]{0:T(128)S(1)}, f32[3]{0:T(128)}, u32[]{:S(2)}) copy-start(f32[3]{0:T(128)} %constant.258.clone) | copy-start | bytes 40
  407.2 6.3 copy-start.15
  408.7 4.9 copy-start.16
  420.9 2.3 copy-start.42
  420.9 2.8 copy-start.28
  420.9 2.8 copy-start.27
  421.0 2.9 copy-start.35
  421.0 2.9 copy-start.11
  421.0 39.9 %copy-start.20 = (f32[2048]{0:T(1024)S(1)}, f32[2048]{0:T(1024)}, u32[]{:S(2)}) copy-start(f32[2048]{0:T(1024)} %copy-done.19) | copy-start | bytes 24580
  425.7 281.7 %copy-start.13 = (f32[1,1,221472]{2,1,0:T(1,128)S(1)}, f32[1,1,221472]{2,1,0:T(1,128)}, u32[]{:S(2)}) copy-start(f32[1,1,221472]{2,1,0:T(1,128)} %param.34) | copy-start | bytes 2657668
  460.9 255.6 %copy-start.1 = (bf16[768,768]{1,0:T(8,128)(2,1)S(1)}, bf16[768,768]{1,0:T(8,128)(2,1)}, u32[]{:S(2)}) copy-start(bf16[768,768]{1,0:T(8,128)(2,1)} %param.25) | copy-start | bytes 3538948
  (5 other events, 7.7 us)
Sparse Core Ops, SparseCore 0:
  57.0 71.1 all-reduce.14
  147.7 68.5 all-reduce.16
  244.2 68.5 all-reduce.18
  392.3 68.5 all-reduce.20
  465.2 232.3 all-reduce.22
where the time goes:
time: 732 us; the launch traced here: 723 us
  waiting for transfers between devices  415 us (57%)
  matrix products  96 us (13%)
  other arithmetic  87.5 us (12%)
  local copies, waits for them, and re-layouts  64.3 us (9%)
  blocking collectives  39.8 us (5%)
  between operations  14.8 us (2%)
    unnamed x6, waiting for transfers between devices  188 us
    psum x1, waiting for transfers between devices, body(): attn = lax.psum(attn_part, 'mp').astype(jnp.float32)  69.8 us
    psum x1, waiting for transfers between devices, body(): ffn = lax.psum(down_part, 'mp').astype(jnp.float32)  64.5 us
    psum x1, waiting for transfers between devices, body(): dx_one = dz_two + lax.psum(back_one, 'mp').astype(jnp.float32)  56.8 us
    unnamed x1, blocking collectives  39.8 us
    psum x1, waiting for transfers between devices, body(): grad_input = dz_one + lax.psum(back_zero, 'mp').astype(jnp.float32)  35.2 us
    reduce_sum x4, other arithmetic, layer_norm(): centered = z - jnp.mean(z, axis=-1, keepdims=True)  20.3 us
    unnamed x108, local copies, waits for them, and re-layouts  19.8 us
  transfers between devices with their start and end apart: 5, of which 5 were waited for; matrix products, arithmetic and copies ran while one was open for 8% of the time, Pallas kernels for 0%

commit v1 on v0

--- a/solution.py
+++ b/solution.py
@@ -192,7 +192,8 @@
         + jnp.dot(d_keys, qkv_weight[1].T, preferred_element_type=jnp.float32)
         + jnp.dot(d_values, qkv_weight[2].T, preferred_element_type=jnp.float32)
     ).astype(jnp.bfloat16)
-    grad_input = dz_one + lax.psum(back_zero, "mp").astype(jnp.float32)
+    time_halves = lambda incoming_x: lax.all_gather(incoming_x, axis_name="mp").sum(axis=0)
+    grad_input = dz_one + time_halves(back_zero).astype(jnp.float32)
     g_vec = jnp.stack(
         [d_gain_one, d_shift_one, d_gain_two, d_shift_two, d_bias_out, d_bias_two]
     ).reshape(-1)

time: 732 us -> 794 us (1.085)
  waiting for transfers between devices: 415 us -> 475 us
  other arithmetic: 87.5 us -> 96.7 us
    all_gather x0 -> x1, waiting for transfers between devices: none -> 73.5 us  [body(): lax.all_gather(incoming_x, axis_name='mp').sum(axis=0)]
    psum x1 -> x0, waiting for transfers between devices: 35.2 us -> none  [body(): grad_input = dz_one + lax.psum(back_zero, 'mp').astype(jnp.float32)]
    unnamed x6, waiting for transfers between devices: 188 us -> 222 us
    psum x1, waiting for transfers between devices: 56.8 us -> 44.7 us  [body(): dx_one = dz_two + lax.psum(back_one, 'mp').astype(jnp.float32)]
    reduce_sum x0 -> x1, other arithmetic: none -> 8.97 us  [body(): lax.all_gather(incoming_x, axis_name='mp').sum(axis=0)]
    unnamed x108 -> x114, local copies, waits for them, and re-layouts: 19.8 us -> 17.6 us
  transfers between devices with their start and end apart: 5 -> 5, of which waited for: 5 -> 5; matrix products, arithmetic and copies ran while one was open for 8% -> 6% of each run, Pallas kernels for 0% -> 0%
where the time goes in v1:
time: 794 us; the launch traced here: 785 us
  waiting for transfers between devices  475 us (60%)
  other arithmetic  96.7 us (12%)
  matrix products  93.1 us (12%)
  local copies, waits for them, and re-layouts  61.8 us (8%)
  blocking collectives  37.5 us (5%)
  between operations  15 us (2%)
    unnamed x6, waiting for transfers between devices  222 us
    all_gather x1, waiting for transfers between devices, body(): lax.all_gather(incoming_x, axis_name='mp').sum(axis=0)  73.5 us
    psum x1, waiting for transfers between devices, body(): attn = lax.psum(attn_part, 'mp').astype(jnp.float32)  69.8 us
    psum x1, waiting for transfers between devices, body(): ffn = lax.psum(down_part, 'mp').astype(jnp.float32)  64.5 us
    psum x1, waiting for transfers between devices, body(): dx_one = dz_two + lax.psum(back_one, 'mp').astype(jnp.float32)  44.7 us
    unnamed x1, blocking collectives  37.5 us
    reduce_sum x4, other arithmetic, layer_norm(): centered = z - jnp.mean(z, axis=-1, keepdims=True)  20.2 us
    unnamed x114, local copies, waits for them, and re-layouts  17.6 us
  transfers between devices with their start and end apart: 5, of which 5 were waited for; matrix products, arithmetic and copies ran while one was open for 6% of the time, Pallas kernels for 0%

profile of v1, /device:TPU:0, one launch (start us, length us, event | category | flops | bytes accessed | tf_op | source)
XLA Modules:
  0.0 785.5 jit_solution(9939046409115414909)
XLA Ops:
  7.2 4.3 convolution_bitcast_fusion
  13.1 3.1 squeeze.43
  16.2 2.2 squeeze.44
  19.4 2.9 fusion.85
  22.3 28.6 %while.30 = (s32[]{:T(128)}, bf16[4,512,3,64]{1,3,2,0:T(8,128)(2,1)}, f32[4,3,512]{2,1,0:T(4,128)}, bf16[4,512,3,64]{1,3,2,0:T(8,128)(2,1)S(1)}, s32[4]{0:T(128)...) while((s32[]{:T(128)}, ...), condition=%wide.region_5.6_spmd, body=%wide.region_0.5_spmd.sunk | while | flops 208942080 | bytes 11540152 | solution.py:131
  27.8 1.7 fusion.169
  42.1 1.7 fusion.169
  50.9 2.0 copy.76
  53.2 3.7 convolution_convert_fusion.4
  58.4 69.8 %all-reduce.14.cloned.1.call-done = bf16[2048,768]{1,0:T(8,128)(2,1)} async-done(((bf16[2048,768]{1,0:T(8,128)(2,1)}), bf16[2048,768]{1,0:T(8,128)(2,1)}) %all-reduce.14.cloned.1.call-update) | async-done | bytes 3145744 | tf_op jit(solution)/shard_map/psum | solution.py:136
  128.2 4.1 fusion.74
  132.9 1.8 multiply_reduce_fusion.6
  135.3 6.7 multiply_convert_fusion.1
  143.6 3.9 convolution_convert_fusion.3
  151.7 64.5 %all-reduce.16.cloned.1.call-done = bf16[2048,768]{1,0:T(8,128)(2,1)} async-done(((bf16[2048,768]{1,0:T(8,128)(2,1)}), bf16[2048,768]{1,0:T(8,128)(2,1)}) %all-reduce.16.cloned.1.call-update) | async-done | bytes 3145744 | tf_op jit(solution)/shard_map/psum | solution.py:148
  216.2 5.4 fusion.126
  223.5 3.6 multiply_reduce_fusion.1
  227.2 4.7 fusion.125
  232.0 6.4 convert_reduce_fusion
  238.4 1.7 copy-done.47
  240.1 4.0 convolution_convert_fusion.2
  244.6 7.9 %fusion.114 = f32[768,768]{1,0:T(8,128)} fusion(bf16[2048,768]{1,0:T(8,128)(2,1)} %copy-done.48, f32[2048,768]{1,0:T(8,128)} %copy-done.7, f32[2048]{0:T(1024)} %copy-done.23), kind=kOutput, calls=%fused_computation.207 | convolution fusion | flops 2419064832 | bytes 11804672 | tf_op jit(solution)/shard_map/dot_general | solution.py:156
  252.5 3.5 reshape.870
  256.0 8.6 %fusion.117 = f32[768,768]{1,0:T(8,128)} fusion(bf16[2048,768]{1,0:T(8,128)(2,1)} %copy-done.47, f32[768]{0:T(1024)S(1)} %copy-done.32, f32[768]{0:T(1024)S(1)} %get-tuple-element.346, f32[2048]{0:T(1024)S(1)} %copy-done.22, bf16[2048,768]{1,0:T(8,128)(2,1)} %all-reduce.14.cloned.1.call-done, bf16[2048,768]{1,0:T(8,128)(2,1)} %param.20, ...), kind=kOutput, calls=%fused_computation.210 | convolution fusion | flops 2430074880 | bytes 11822080 | tf_op jit(solution)/shard_map/dot_general | solution.py:160
  264.6 3.5 reshape.869
  268.1 44.7 %all-reduce.18.cloned.1.call-done = bf16[2048,768]{1,0:T(8,128)(2,1)} async-done(((bf16[2048,768]{1,0:T(8,128)(2,1)}), bf16[2048,768]{1,0:T(8,128)(2,1)}) %all-reduce.18.cloned.1.call-update) | async-done | bytes 3145744 | tf_op jit(solution)/shard_map/psum | solution.py:166
  312.8 9.8 %multiply_reduce_fusion.2 = (f32[768]{0:T(1024)S(1)}, f32[2048]{0:T(1024)S(1)}, f32[768]{0:T(1024)S(1)}, f32[768]{0:T(1024)S(1)}) fusion(f32[2048]{0:T(1024)S(1)} %copy-done.22, bf16[2048,768]{1,0:T(8,128)(2,1)} %all-reduce.18.cloned.1.call-done, f32[2048,768]{1,0:T(8,128)} %copy-done.7, f32[2048]{0:T(1024)S(1)} %copy-done.24, ...), kind=kLoop, calls=%fused_computation.97 | loop fusion | flops 25161472 | bytes 15776768 | tf_op jit(solution)/shard_map/transpose(jvp())/reduce_sum | solution.py:31
  322.7 6.0 fusion.124
  328.7 2.4 fusion.116
  332.9 2.0 reshape.868
  337.7 43.6 %while.31 = (s32[]{:T(128)}, bf16[4,512,3,64]{1,3,2,0:T(8,128)(2,1)S(1)}, bf16[4,512,3,64]{1,3,2,0:T(8,128)(2,1)}, bf16[4,512,3,64]{1,3,2,0:T(8,128)(2,1)}, bf16...) while((s32[]{:T(128)}, ...), condition=%wide.region_23.24_spmd, body=%wide.region_19.23_spmd.sunk | while | flops 511226880 | bytes 26134740 | solution.py:174
  381.3 2.0 copy.80
  384.2 1.7 copy.81
  389.6 5.6 multiply_bitcast_fusion
  395.2 1.9 copy.85
  397.1 2.2 reshape.867
  403.3 2.0 fusion.94
  406.4 2.8 add_convert_fusion
  409.2 221.9 %all-reduce.20.cloned.1.call-done = (f32[8,55296]{1,0:T(8,128)}, f32[8,18432]{1,0:T(8,128)}, f32[8,73728]{1,0:T(8,128)}, f32[8,73728]{1,0:T(8,128)}) async-done(((f32[8,55296]{1,0:T(8,128)}, f32[8,18432]{1,0:T(8,128)}, f32[8,73728]{1,0:T(8,128)}, f32[8,73728]{1,0:T(8,128)}), (f32[8,55296]{1,0:T(8,128)}, f32[8,18432]{1,0:T(8,128)}, f32[8,73728]{1,0:T(8,128)}, ...) | async-done | bytes 7077904
  631.2 2.2 fusion.101
  633.3 1.7 fusion.102
  635.0 2.4 fusion.92
  637.5 2.8 fusion.91
  640.2 73.5 %all-gather.3.cloned.1.call-done = bf16[8192,768]{1,0:T(8,128)(2,1)} async-done(((bf16[2048,768]{1,0:T(8,128)(2,1)}), bf16[8192,768]{1,0:T(8,128)(2,1)}) %all-gather.3.cloned.1.call-update) | async-done | bytes 12582928 | tf_op jit(solution)/shard_map/all_gather | solution.py:195
  713.7 9.0 %reduce_sum.291 = bf16[2048,768]{1,0:T(8,128)(2,1)} reduce(bf16[4,2048,768]{2,1,0:T(8,128)(2,1)} %bitcast.210, bf16[]{:T(256)} %constant.248.clone.1), dimensions={0}, to_apply=%region_24.25 | reduce | flops 4718592 | bytes 15728642 | tf_op jit(solution)/shard_map/reduce_sum | solution.py:195
  722.7 6.0 add_reduce_fusion
  729.0 37.5 %all-reduce.7 = (f32[8,144]{1,0:T(8,128)S(1)}, f32[8,48]{1,0:T(8,128)S(1)}, f32[8,96]{1,0:T(8,128)S(1)}) all-reduce(f32[8,144]{1,0:T(8,128)S(1)} %reshape.865, f32[8,48]{1,0:T(8,128)S(1)} %reshape.871, f32[8,96]{1,0:T(8,128)S(1)} %reshape.872), channel_id=3, replica_groups=mesh['dp'=8,'mp'=4] {'dp'}, use_global_device_ids=true, to_apply=%region_31.32.clone | all-reduce | flops 2304 | bytes 18432
  769.3 9.2 %multiply_add_fusion.1 = (f32[1,1,221472]{2,1,0:T(1,128)}, f32[1,1,221472]{2,1,0:T(1,128)}, f32[1,1,221472]{2,1,0:T(1,128)}, f32[1,1,221472]{2,1,0:T(1,128)}) fusion(f32[1,1,221472]{2,1,0:T(1,128)S(1)} %copy-done.19, f32[1,1,221472]{2,1,0:T(1,128)} %param.31, f32[1,1,221472]{2,1,0:T(1,128)S(1)} %dynamic-update-slice.6, f32[1,1,221472]{2,1,0:T(1,128)} %param.32, ...), kind=kLoop, calls=%fused_computation.144 | loop fusion | flops 3986496 | bytes 7972992 | tf_op jit(solution)/shard_map/add | solution.py:225
  (272 shorter events, 93.7 us)
Async XLA Ops:
  7.2 128.1 %copy-start = (bf16[768,768]{1,0:T(8,128)(2,1)S(1)}, bf16[768,768]{1,0:T(8,128)(2,1)}, u32[]{:S(2)}) copy-start(bf16[768,768]{1,0:T(8,128)(2,1)} %param.25) | copy-start | bytes 3538948
  7.2 121.0 %all-reduce.14.cloned.1.call-start = ((), (), s32[]{:S(2)}) async-start(), calls=%async_computation | async-start | bytes 6291456 | tf_op jit(solution)/shard_map/psum | solution.py:136
  11.5 6.9 copy-start.40
  16.2 6.1 copy-start.43
  50.9 2.0 copy-start.14
  53.0 4.2 copy-start.34
  53.0 4.2 copy-start.39
  56.9 159.4 %all-reduce.16.cloned.1.call-start = ((), (), s32[]{:S(2)}) async-start(), calls=%async_computation.1 | async-start | bytes 6291456 | tf_op jit(solution)/shard_map/psum | solution.py:148
  128.2 4.1 copy-start.3
  128.2 4.7 copy-start.5
  128.2 7.1 copy-start.31
  128.2 7.1 copy-start.36
  135.2 6.7 copy-start.21
  135.3 8.3 %copy-start.41 = (bf16[768,768]{1,0:T(8,128)(2,1)S(1)}, bf16[768,768]{1,0:T(8,128)(2,1)}, u32[]{:S(2)}) copy-start(bf16[768,768]{1,0:T(8,128)(2,1)} %param.27) | copy-start | bytes 3538948
  147.5 165.3 %all-reduce.18.cloned.1.call-start = ((), (), s32[]{:S(2)}) async-start(), calls=%async_computation.2 | async-start | bytes 6291456 | tf_op jit(solution)/shard_map/psum | solution.py:166
  221.6 1.9 copy-start.9
  222.5 4.7 copy-start.33
  223.5 8.4 %slice-start = ((s8[6291456]{0:T(1024)(128)(4,1)}), s8[4194304]{0:T(1024)(128)(4,1)S(1)}, s32[]{:S(2)}) async-start(s8[6291456]{0:T(1024)(128)(4,1)} %bitcast.222), calls=%async_computation.5 | async-start | bytes 8388608
  227.2 4.8 copy-start.37
  227.2 4.8 copy-start.42
  227.2 4.8 slice-start.1
  232.0 6.4 copy-start.7
  232.0 6.4 copy-start.23
  244.1 11.9 %copy-start.22 = (f32[2048]{0:T(1024)S(1)}, f32[2048]{0:T(1024)}, u32[]{:S(2)}) copy-start(f32[2048]{0:T(1024)} %copy-done.21) | copy-start | bytes 24580
  244.1 11.9 %copy-start.32 = (f32[768]{0:T(1024)S(1)}, f32[768]{0:T(1024)}, u32[]{:S(2)}) copy-start(f32[768]{0:T(1024)} %get-tuple-element.345) | copy-start | bytes 9220
  244.1 387.1 %all-reduce.20.cloned.1.call-start = ((), (), s32[]{:S(2)}) async-start(), calls=%async_computation.4 | async-start | bytes 14155776
  256.0 56.8 %copy-start.24 = (f32[2048]{0:T(1024)S(1)}, f32[2048]{0:T(1024)}, u32[]{:S(2)}) copy-start(f32[2048]{0:T(1024)} %copy-done.23) | copy-start | bytes 24580
  268.1 54.5 %copy-start.27 = (f32[2048]{0:T(1024)S(1)}, f32[2048]{0:T(1024)}, u32[]{:S(2)}) copy-start(f32[2048]{0:T(1024)} %copy-done.26) | copy-start | bytes 24580
  312.8 9.8 %copy-start.4 = (bf16[2048,768]{1,0:T(8,128)(2,1)S(1)}, bf16[2048,768]{1,0:T(8,128)(2,1)}, u32[]{:S(2)}) copy-start(bf16[2048,768]{1,0:T(8,128)(2,1)} %param.20) | copy-start | bytes 9437188
  312.8 9.9 %copy-start.6 = (bf16[2048,768]{1,0:T(8,128)(2,1)S(1)}, bf16[2048,768]{1,0:T(8,128)(2,1)}, u32[]{:S(2)}) copy-start(bf16[2048,768]{1,0:T(8,128)(2,1)} %all-reduce.14.cloned.1.call-done) | copy-start | bytes 9437188
  312.8 9.9 %copy-start.8 = (bf16[2048,768]{1,0:T(8,128)(2,1)S(1)}, bf16[2048,768]{1,0:T(8,128)(2,1)}, u32[]{:S(2)}) copy-start(bf16[2048,768]{1,0:T(8,128)(2,1)} %all-reduce.18.cloned.1.call-done) | copy-start | bytes 9437188
  328.7 2.9 copy-start.2
  328.7 2.9 copy-start.18
  331.6 6.1 copy-start.15
  331.6 6.1 copy-start.44
  381.3 8.3 %copy-start.16 = (bf16[4,512,3,64]{1,3,2,0:T(8,128)(2,1)}, bf16[4,512,3,64]{1,3,2,0:T(8,128)(2,1)S(1)}, u32[]{:S(2)}) copy-start(bf16[4,512,3,64]{1,3,2,0:T(8,128)(2,1)S(1)} %get-tuple-element.256) | copy-start | bytes 2359300
  381.3 8.3 %copy-start.46 = (f32[3]{0:T(128)S(1)}, f32[3]{0:T(128)}, u32[]{:S(2)}) copy-start(f32[3]{0:T(128)} %constant.259.clone) | copy-start | bytes 40
  397.1 2.6 copy-start.45
  397.1 3.1 copy-start.30
  397.1 3.1 copy-start.29
  397.1 3.7 copy-start.38
  399.3 3.4 copy-start.11
  399.3 3.6 copy-start.13
  399.3 314.4 %all-gather.3.cloned.1.call-start = ((), (), s32[]{:S(2)}) async-start(), calls=%async_computation.3 | async-start | bytes 15728640 | tf_op jit(solution)/shard_map/all_gather | solution.py:195
  403.1 2.3 copy-start.20
  722.7 6.0 copy-start.35
  722.7 46.6 %copy-start.19 = (f32[1,1,221472]{2,1,0:T(1,128)S(1)}, f32[1,1,221472]{2,1,0:T(1,128)}, u32[]{:S(2)}) copy-start(f32[1,1,221472]{2,1,0:T(1,128)} %param.34) | copy-start | bytes 2657668
  722.7 55.7 %copy-start.1 = (bf16[768,768]{1,0:T(8,128)(2,1)S(1)}, bf16[768,768]{1,0:T(8,128)(2,1)}, u32[]{:S(2)}) copy-start(bf16[768,768]{1,0:T(8,128)(2,1)} %param.25) | copy-start | bytes 3538948
  (8 other events, 11.6 us)
Sparse Core Ops, SparseCore 0:
  57.0 71.1 all-reduce.13
  147.7 68.5 all-reduce.15
  244.2 68.5 all-reduce.17
  399.5 231.6 all-reduce.19
  632.6 81.1 all-gather.2
